TPU v7x, 512 devices: a whole 4x8x8 slice. The times are simulated.
512 devices in a mesh: tm: 64 (over z, y), state: 8 (over x, core).
Axes of the slice: x: 4, y: 8, z: 8, core: 2. Of those that a mesh axis runs over, the one named last changes fastest.
Arguments:
- offsets: int32 [5], replicated, may hold values from -3 to 3
- coefficients: float32 [5, 2048], replicated, may hold values from 0.1 to 1
- gain_matrix: bfloat16 [64, 1, 2048, 512], P('tm', None, 'state'), may hold values from -0.0625 to 0.0625
- direct_gain: float32 [64, 1, 512], P('tm'), may hold values from 0.2 to 0.8
- observed_cells: int32 [64, 1, 512], P('tm'), may hold values from 0 to 2047
- observed_values: float32 [64, 1, 512], P('tm'), may hold values from -4 to 4
Outputs:
- transition: float32 [64, 2048, 2048], P('tm', None, 'state')
- offset_term: float32 [64, 2048], P('tm')
All inputs are finite; a program needn't handle non-finite values.
Results may differ from a plain program's by a relative error of at most 0.0036.
Values may be sent and summed in bfloat16 or wider, within the bound.
A program may use at most 64 MiB of HBM per device.

v0:
```python
import jax
import jax.numpy as jnp
from jax import lax
from jax.sharding import PartitionSpec as P


def from_behind(value, axis, steps):
    count = lax.axis_size(axis)
    leading, last = (max(0, -steps), min(count, count - steps))
    return lax.ppermute(value, axis, [(source, source + steps) for source in range(leading, last)])


def advance(matrix, step_gains, cells_used, weights, offsets, forcing):
    spread = weights[0][:, None] * jnp.roll(matrix, -offsets[0], axis=0)
    for tap_index in range(1, weights.shape[0]):
        spread = spread + weights[tap_index][:, None] * jnp.roll(
            matrix, -offsets[tap_index], axis=0
        )
    picked = jnp.take(spread, cells_used[0], axis=0)
    if forcing is not None:
        picked = picked - forcing[0][:, None]
    correction = jnp.dot(
        step_gains[0], picked.astype(jnp.bfloat16), preferred_element_type=jnp.float32
    )
    matrix = spread - correction
    return matrix


def local_gain_rows(gain_matrix, direct_gain, observed_cells):
    row_count = gain_matrix.shape[2]
    first_row = lax.axis_index("state") * row_count
    cell_ids = first_row + lax.broadcasted_iota(jnp.int32, gain_matrix.shape[1:], 1)
    observed_hit = cell_ids == observed_cells[0][:, None, :]
    extra = jnp.where(
        observed_hit, direct_gain[0][:, None, :], jnp.zeros_like(direct_gain[0][:, None, :])
    )
    return (gain_matrix[0].astype(jnp.float32) + extra).astype(jnp.bfloat16)


def shards(offsets, coefficients, gain_matrix, direct_gain, observed_cells, observed_values):
    weights = coefficients / jnp.sum(coefficients, axis=0, keepdims=True)
    gain_rows = local_gain_rows(gain_matrix, direct_gain, observed_cells)
    gain_full = lax.all_gather(gain_rows, "state", axis=1, tiled=True)
    cells_used = observed_cells[0]
    forcing = observed_values[0]
    cell_count = gain_full.shape[1]
    columns = gain_rows.shape[1]
    first_column = lax.axis_index("state") * columns
    row_ids = lax.broadcasted_iota(jnp.int32, (cell_count, columns), 0)
    column_ids = first_column + lax.broadcasted_iota(jnp.int32, (cell_count, columns), 1)
    identity_panel = (row_ids == column_ids).astype(jnp.float32)
    span_index = lax.axis_index("tm")

    def own_map(matrix, forced_values=None):
        return advance(matrix, gain_full, cells_used, weights, offsets, forced_values)

    level_zero_trans = own_map(identity_panel)
    level_zero_shift = own_map(jnp.zeros((cell_count, 1), jnp.float32), forcing)
    left_trans, left_shift = from_behind((level_zero_trans, level_zero_shift), "tm", 1)
    level_one_trans = jnp.where(span_index >= 1, own_map(left_trans), level_zero_trans)
    level_one_shift = jnp.where(
        span_index >= 1, own_map(left_shift) + level_zero_shift, level_zero_shift
    )
    far_trans, far_shift = from_behind((level_one_trans, level_one_shift), "tm", 2)
    far_trans = jnp.where(span_index == 1, identity_panel, far_trans)
    earlier_gains, earlier_cells = from_behind((gain_full, cells_used), "tm", 1)
    carried_trans = own_map(
        advance(far_trans, earlier_gains, earlier_cells, weights, offsets, None)
    )
    carried_shift = own_map(
        advance(far_shift, earlier_gains, earlier_cells, weights, offsets, None)
    )
    first_carried = 1
    transition = jnp.where(span_index >= first_carried, carried_trans, level_one_trans)
    offset_term = jnp.where(span_index >= 2, carried_shift + level_one_shift, level_one_shift)
    return (transition[None], offset_term[:, 0][None])


def solution(mesh):
    in_specs = (
        P(),
        P(),
        P("tm", None, "state", None),
        P("tm", None, None),
        P("tm", None, None),
        P("tm", None, None),
    )
    out_specs = (P("tm", None, "state"), P("tm", None))
    return jax.shard_map(shards, mesh=mesh, in_specs=in_specs, out_specs=out_specs, check_vma=False)
```

profile of v0, /device:TPU:25, one launch (start us, length us, event | category | flops | bytes accessed | tf_op | source)
XLA Modules:
  0.0 282.2 jit_solution(14787118618400152176)
XLA Ops:
  7.2 1.8 fusion.67
  9.1 4.4 %collective-permute-start.3 = (s32[1,512]{1,0:T(1,128)}, s32[1,512]{1,0:T(1,128)S(1)}, u32[]{:S(2)}, u32[]{:S(2)}) collective-permute-start(s32[1,512]{1,0:T(1,128)} %bitcast.144), channel_id=1, source_target_pairs={{0,8},{8,16},{16,24},{24,32},{32,40},{40,48},{48,56},{56,64},{64,7... | collective-permute-start | bytes 6152 | tf_op jit(solution)/shard_map/ppermute | solution.py:10
  13.5 1.5 fusion.131
  21.0 5.6 %fusion.42 = f32[2048,256]{1,0:T(8,128)S(1)} fusion(s32[]{:T(128)S(6)} %select_n.189, f32[2048,256]{1,0:T(8,128)S(1)} %fusion.66, s32[]{:T(128)S(6)} %select_n.181, s32[]{:T(128)S(6)} %select_n.183, s32[]{:T(128)S(6)} %select_n.185, s32[]{:T(128)S(6)} %select_n.187, f32[2048]{0:T(1024)S(1)} %bitcast.127, f32[2048]{0:T(1024)S(1)} %bitcast.131, ...), kind=kLoop, calls=%fused_computation.88 | loop fusion | flops 7340032 | bytes 4235284 | tf_op jit(solution)/shard_map/add | solution.py:16
  26.7 1.6 gather_fusion
  28.7 3.1 %gather_fusion.4 = f32[512]{0:T(512)S(1)} fusion(f32[2048]{0:T(1024)S(1)} %bitcast.119, s32[1024]{0:T(1024)S(1)} %pad_clamp_fusion.1), kind=kCustom, calls=%fused_computation.1.clone | custom fusion | bytes 6144 | tf_op jit(solution)/shard_map/jit(_take)/gather | solution.py:19
  31.8 13.6 %all-gather.2.cloned.1.call-done = bf16[1,2048,512]{2,1,0:T(8,128)(2,1)} async-done(((bf16[1,256,512]{2,1,0:T(8,128)(2,1)}), bf16[1,2048,512]{2,1,0:T(8,128)(2,1)}) %all-gather.2.cloned.1.call-update) | async-done | bytes 2097168 | tf_op jit(solution)/shard_map/all_gather | solution.py:43
  45.5 4.5 %convolution_subtract_fusion.3 = f32[2048,256]{1,0:T(8,128)} fusion(f32[2048,256]{1,0:T(8,128)} %copy-done.1, bf16[1,2048,512]{2,1,0:T(8,128)(2,1)} %all-gather.2.cloned.1.call-done, bf16[512,256]{1,0:T(8,128)(2,1)S(1)} %gather_fusion, pred[512]{0:T(512)(128)(4,1)S(1)} %get-tuple-element.9), kind=kOutput, calls=%fused_computation.43 | convolution fusion | flops 537526272 | bytes 6554112 | tf_op jit(solution)/shard_map/dot_general | solution.py:22
  50.0 4.3 %collective-permute-start = (f32[2048,256]{1,0:T(8,128)}, f32[2048,256]{1,0:T(8,128)}, u32[]{:S(2)}, u32[]{:S(2)}) collective-permute-start(f32[2048,256]{1,0:T(8,128)} %convolution_subtract_fusion.3), channel_id=1, source_target_pairs={{0,8},{8,16},{16,24},{24,32},{32,40},{40,48},{48,56},{56,64},{64,7... | collective-permute-start | bytes 6291464 | tf_op jit(solution)/shard_map/ppermute | solution.py:10
  55.0 2.2 collective-permute-start.4
  57.2 42.2 %collective-permute-done.4 = f32[2048,1]{0,1:T(1,128)S(1)} collective-permute-done((f32[2048,1]{0,1:T(1,128)S(1)}, f32[2048,1]{0,1:T(1,128)S(1)}, u32[]{:S(2)}, u32[]{:S(2)}) %collective-permute-start.4) | collective-permute-done | bytes 8224 | tf_op jit(solution)/shard_map/ppermute | solution.py:10
  99.6 3.1 %gather_fusion.5 = f32[512]{0:T(512)S(1)} fusion(f32[2048]{0:T(1024)S(1)} %bitcast.122, s32[1024]{0:T(1024)S(1)} %pad_clamp_fusion.1), kind=kCustom, calls=%fused_computation.5.clone | custom fusion | bytes 6144 | tf_op jit(solution)/shard_map/jit(_take)/gather | solution.py:19
  103.4 4.2 %collective-permute-start.5 = (f32[2048,1]{0,1:T(1,128)S(1)}, f32[2048,1]{0,1:T(1,128)S(1)}, u32[]{:S(2)}, u32[]{:S(2)}) collective-permute-start(f32[2048,1]{0,1:T(1,128)S(1)} %fusion.10), channel_id=1, source_target_pairs={{0,16},{8,24},{16,32},{24,40},{32,48},{40,56},{48,64},{56,72},{64,... | collective-permute-start | bytes 24584 | tf_op jit(solution)/shard_map/ppermute | solution.py:10
  107.7 3.1 %collective-permute-start.2 = (bf16[1,2048,512]{2,1,0:T(8,128)(2,1)S(1)}, bf16[1,2048,512]{2,1,0:T(8,128)(2,1)}, u32[]{:S(2)}, u32[]{:S(2)}) collective-permute-start(bf16[1,2048,512]{2,1,0:T(8,128)(2,1)S(1)} %copy-done), channel_id=1, source_target_pairs={{0,8},{8,16},{16,24},{24,32},{32,40},{40,48},{48,56},{56,64},{64,7... | collective-permute-start | bytes 6291464 | tf_op jit(solution)/shard_map/ppermute | solution.py:10
  110.8 1.7 constant_dynamic-update-slice_fusion.1
  112.6 1.7 constant_dynamic-update-slice_fusion
  114.3 3.1 %fusion.62 = f32[2048,256]{1,0:T(8,128)} fusion(f32[4096,256]{1,0:T(8,128)S(1)} %constant_dynamic-update-slice_fusion, s32[]{:T(128)S(6)} %select_n.189, s32[]{:T(128)S(6)} %select_n.187, s32[]{:T(128)S(6)} %select_n.185, s32[]{:T(128)S(6)} %select_n.183, s32[]{:T(128)S(6)} %select_n.181, f32[2048]{0:T(1024)S(1)} %bitcast.128, f32[2048]{0:T(1024)S(1)} %bitcast.132, ...), kind=kLoop, calls=%fused_computation.109 | loop fusion | flops 4718592 | bytes 12623892 | tf_op jit(solution)/shard_map/add | solution.py:16
  117.4 3.1 %gather_fusion.1 = bf16[512,256]{1,0:T(8,128)(2,1)S(1)} fusion(f32[2048,256]{1,0:T(8,128)} %fusion.62, s32[1024]{0:T(1024)S(1)} %pad_clamp_fusion.1), kind=kCustom, calls=%fused_computation.2.clone | custom fusion | bytes 526336 | tf_op jit(solution)/shard_map/jit(_take)/gather | solution.py:19
  120.5 3.7 %fusion.1 = f32[2048,256]{1,0:T(8,128)} fusion(f32[2048,256]{1,0:T(8,128)} %convolution_subtract_fusion.3, f32[2048,256]{1,0:T(8,128)} %fusion.62, bf16[1,2048,512]{2,1,0:T(8,128)(2,1)S(1)} %copy-done, pred[]{:T(512)S(6)} %ge.18, bf16[512,256]{1,0:T(8,128)(2,1)S(1)} %gather_fusion.1, pred[512]{0:T(512)(128)(4,1)S(1)} %get-tuple-element.9), kind=kOutput, calls=%fused_computation.42 | convolution fusion | flops 538050560 | bytes 8651265 | tf_op jit(solution)/shard_map/dot_general | solution.py:22
  124.3 4.5 %collective-permute-start.1 = (f32[2048,256]{1,0:T(8,128)}, f32[2048,256]{1,0:T(8,128)}, u32[]{:S(2)}, u32[]{:S(2)}) collective-permute-start(f32[2048,256]{1,0:T(8,128)} %fusion.1), channel_id=1, source_target_pairs={{0,16},{8,24},{16,32},{24,40},{32,48},{40,56},{48,64},{56,72},{64,... | collective-permute-start | bytes 6291464 | tf_op jit(solution)/shard_map/ppermute | solution.py:10
  129.0 3.1 %gather_fusion.6 = f32[512]{0:T(512)S(1)} fusion(f32[2048]{0:T(1024)S(1)} %bitcast.120, s32[1024]{0:T(1024)S(1)} %pad_clamp_fusion), kind=kCustom, calls=%fused_computation.6.clone | custom fusion | bytes 6144 | tf_op jit(solution)/shard_map/jit(_take)/gather | solution.py:19
  132.2 24.6 %collective-permute-done.2 = bf16[1,2048,512]{2,1,0:T(8,128)(2,1)} collective-permute-done((bf16[1,2048,512]{2,1,0:T(8,128)(2,1)S(1)}, bf16[1,2048,512]{2,1,0:T(8,128)(2,1)}, u32[]{:S(2)}, u32[]{:S(2)}) %collective-permute-start.2) | collective-permute-done | bytes 2097184 | tf_op jit(solution)/shard_map/ppermute | solution.py:10
  156.7 2.2 fusion.7
  159.4 3.1 %gather_fusion.7 = f32[512]{0:T(512)S(1)} fusion(f32[2048]{0:T(1024)S(1)} %bitcast.121, s32[1024]{0:T(1024)S(1)} %pad_clamp_fusion.1), kind=kCustom, calls=%fused_computation.7.clone | custom fusion | bytes 6144 | tf_op jit(solution)/shard_map/jit(_take)/gather | solution.py:19
  163.8 83.7 %collective-permute-done.1 = f32[2048,256]{1,0:T(8,128)} collective-permute-done((f32[2048,256]{1,0:T(8,128)}, f32[2048,256]{1,0:T(8,128)}, u32[]{:S(2)}, u32[]{:S(2)}) %collective-permute-start.1) | collective-permute-done | bytes 2097184 | tf_op jit(solution)/shard_map/ppermute | solution.py:10
  247.5 1.9 broadcast_select_fusion
  249.4 6.4 %fusion.28 = f32[2048,256]{1,0:T(8,128)} fusion(s32[]{:T(128)S(6)} %select_n.189, f32[2048,256]{1,0:T(8,128)S(1)} %broadcast_select_fusion, s32[]{:T(128)S(6)} %select_n.181, s32[]{:T(128)S(6)} %select_n.183, s32[]{:T(128)S(6)} %select_n.185, s32[]{:T(128)S(6)} %select_n.187, f32[2048]{0:T(1024)S(1)} %bitcast.129, f32[2048]{0:T(1024)S(1)} %bitcast.133, ...), kind=kLoop, calls=%fused_computation.74 | loop fusion | flops 7340032 | bytes 4235284 | tf_op jit(solution)/shard_map/add | solution.py:16
  255.8 3.1 %gather_fusion.2 = bf16[512,256]{1,0:T(8,128)(2,1)S(1)} fusion(f32[2048,256]{1,0:T(8,128)} %fusion.28, s32[1024]{0:T(1024)S(1)} %pad_clamp_fusion), kind=kCustom, calls=%fused_computation.3.clone | custom fusion | bytes 526336 | tf_op jit(solution)/shard_map/jit(_take)/gather | solution.py:19
  259.0 3.0 %convolution_subtract_fusion.1 = f32[2048,256]{1,0:T(8,128)S(1)} fusion(f32[2048,256]{1,0:T(8,128)} %fusion.28, bf16[1,2048,512]{2,1,0:T(8,128)(2,1)} %collective-permute-done.2, bf16[512,256]{1,0:T(8,128)(2,1)S(1)} %gather_fusion.2, pred[512]{0:T(512)(128)(4,1)S(1)} %get-tuple-element.6), kind=kOutput, calls=%fused_computation.40 | convolution fusion | flops 537526272 | bytes 6554112 | tf_op jit(solution)/shard_map/dot_general | solution.py:22
  262.0 6.4 %fusion.14 = f32[2048,256]{1,0:T(8,128)} fusion(s32[]{:T(128)S(6)} %select_n.189, f32[2048,256]{1,0:T(8,128)S(1)} %convolution_subtract_fusion.1, s32[]{:T(128)S(6)} %select_n.181, s32[]{:T(128)S(6)} %select_n.183, s32[]{:T(128)S(6)} %select_n.185, s32[]{:T(128)S(6)} %select_n.187, f32[2048]{0:T(1024)S(1)} %bitcast.130, f32[2048]{0:T(1024)S(1)} %bitcast.134, ...), kind=kLoop, calls=%fused_computation.60 | loop fusion | flops 7340032 | bytes 4235284 | tf_op jit(solution)/shard_map/add | solution.py:16
  268.4 3.1 %gather_fusion.3 = bf16[512,256]{1,0:T(8,128)(2,1)S(1)} fusion(f32[2048,256]{1,0:T(8,128)} %fusion.14, s32[1024]{0:T(1024)S(1)} %pad_clamp_fusion.1), kind=kCustom, calls=%fused_computation.4.clone | custom fusion | bytes 526336 | tf_op jit(solution)/shard_map/jit(_take)/gather | solution.py:19
  271.6 3.7 %fusion.2 = f32[1,2048,256]{2,1,0:T(8,128)} fusion(f32[2048,256]{1,0:T(8,128)} %fusion.1, f32[2048,256]{1,0:T(8,128)} %fusion.14, bf16[1,2048,512]{2,1,0:T(8,128)(2,1)S(1)} %copy-done, pred[]{:T(512)S(6)} %ge.18, bf16[512,256]{1,0:T(8,128)(2,1)S(1)} %gather_fusion.3, pred[512]{0:T(512)(128)(4,1)S(1)} %get-tuple-element.9), kind=kOutput, calls=%fused_computation.44 | convolution fusion | flops 538050560 | bytes 8651265 | tf_op jit(solution)/shard_map/dot_general | solution.py:22
  (38 shorter events, 6.4 us)
Async XLA Ops:
  7.2 38.3 %all-gather.2.cloned.1.call-start = ((), (), s32[]{:S(2)}) async-start(), calls=%async_computation | async-start | bytes 2359296 | tf_op jit(solution)/shard_map/all_gather | solution.py:43
  9.1 48.1 %collective-permute-start.3 = (s32[1,512]{1,0:T(1,128)}, s32[1,512]{1,0:T(1,128)S(1)}, u32[]{:S(2)}, u32[]{:S(2)}) collective-permute-start(s32[1,512]{1,0:T(1,128)} %bitcast.144), channel_id=1, source_target_pairs={{0,8},{8,16},{16,24},{24,32},{32,40},{40,48},{48,56},{56,64},{64,7... | collective-permute-start | bytes 6152 | tf_op jit(solution)/shard_map/ppermute | solution.py:10
  26.7 5.1 %copy-start.1 = (f32[2048,256]{1,0:T(8,128)}, f32[2048,256]{1,0:T(8,128)S(1)}, u32[]{:S(2)}) copy-start(f32[2048,256]{1,0:T(8,128)S(1)} %fusion.42) | copy-start | bytes 6291460
  26.7 5.1 %copy-start.2 = (s32[1,1,512]{2,1,0:T(1,128)S(1)}, s32[1,1,512]{2,1,0:T(1,128)}, u32[]{:S(2)}) copy-start(s32[1,1,512]{2,1,0:T(1,128)} %param.18) | copy-start | bytes 6148
  45.5 8.8 %copy-start = (bf16[1,2048,512]{2,1,0:T(8,128)(2,1)S(1)}, bf16[1,2048,512]{2,1,0:T(8,128)(2,1)}, u32[]{:S(2)}) copy-start(bf16[1,2048,512]{2,1,0:T(8,128)(2,1)} %all-gather.2.cloned.1.call-done) | copy-start | bytes 6291460
  45.5 8.8 %copy-start.3 = (f32[1,1,512]{2,1,0:T(1,128)S(1)}, f32[1,1,512]{2,1,0:T(1,128)}, u32[]{:S(2)}) copy-start(f32[1,1,512]{2,1,0:T(1,128)} %param.19) | copy-start | bytes 6148
  50.0 60.8 %collective-permute-start = (f32[2048,256]{1,0:T(8,128)}, f32[2048,256]{1,0:T(8,128)}, u32[]{:S(2)}, u32[]{:S(2)}) collective-permute-start(f32[2048,256]{1,0:T(8,128)} %convolution_subtract_fusion.3), channel_id=1, source_target_pairs={{0,8},{8,16},{16,24},{24,32},{32,40},{40,48},{48,56},{56,64},{64,7... | collective-permute-start | bytes 6291464 | tf_op jit(solution)/shard_map/ppermute | solution.py:10
  55.0 44.5 %collective-permute-start.4 = (f32[2048,1]{0,1:T(1,128)S(1)}, f32[2048,1]{0,1:T(1,128)S(1)}, u32[]{:S(2)}, u32[]{:S(2)}) collective-permute-start(f32[2048,1]{0,1:T(1,128)S(1)} %fusion.11), channel_id=1, source_target_pairs={{0,8},{8,16},{16,24},{24,32},{32,40},{40,48},{48,56},{56,64},{64,7... | collective-permute-start | bytes 24584 | tf_op jit(solution)/shard_map/ppermute | solution.py:10
  103.4 7.4 %collective-permute-start.5 = (f32[2048,1]{0,1:T(1,128)S(1)}, f32[2048,1]{0,1:T(1,128)S(1)}, u32[]{:S(2)}, u32[]{:S(2)}) collective-permute-start(f32[2048,1]{0,1:T(1,128)S(1)} %fusion.10), channel_id=1, source_target_pairs={{0,16},{8,24},{16,32},{24,40},{32,48},{40,56},{48,64},{56,72},{64,... | collective-permute-start | bytes 24584 | tf_op jit(solution)/shard_map/ppermute | solution.py:10
  107.7 49.1 %collective-permute-start.2 = (bf16[1,2048,512]{2,1,0:T(8,128)(2,1)S(1)}, bf16[1,2048,512]{2,1,0:T(8,128)(2,1)}, u32[]{:S(2)}, u32[]{:S(2)}) collective-permute-start(bf16[1,2048,512]{2,1,0:T(8,128)(2,1)S(1)} %copy-done), channel_id=1, source_target_pairs={{0,8},{8,16},{16,24},{24,32},{32,40},{40,48},{48,56},{56,64},{64,7... | collective-permute-start | bytes 6291464 | tf_op jit(solution)/shard_map/ppermute | solution.py:10
  124.3 123.2 %collective-permute-start.1 = (f32[2048,256]{1,0:T(8,128)}, f32[2048,256]{1,0:T(8,128)}, u32[]{:S(2)}, u32[]{:S(2)}) collective-permute-start(f32[2048,256]{1,0:T(8,128)} %fusion.1), channel_id=1, source_target_pairs={{0,16},{8,24},{16,32},{24,40},{32,48},{40,56},{48,64},{56,72},{64,... | collective-permute-start | bytes 6291464 | tf_op jit(solution)/shard_map/ppermute | solution.py:10
Sparse Core Ops, SparseCore 0:
  10.1 35.2 all-gather.1
where the time goes:
time: 284 us; the launch traced here: 282 us
  waiting for transfers between devices  164 us (58%)
  other arithmetic  29 us (10%)
  local copies, waits for them, and re-layouts  28.6 us (10%)
  starting transfers between devices  22.8 us (8%)
  matrix products  19.8 us (7%)
  between operations  17.7 us (6%)
    ppermute x6, waiting for transfers between devices, from_behind(): lax.ppermute(value, axis, [(source, source + steps) for source in range(l...  151 us
    gather x8, local copies, waits for them, and re-layouts, advance(): picked = jnp.take(spread, cells_used[0], axis=0)  23.6 us
    ppermute x6, starting transfers between devices, from_behind(): lax.ppermute(value, axis, [(source, source + steps) for source in range(l...  22.8 us
    add x8, other arithmetic, advance(): spread + weights[tap_index][:, None] * jnp.roll(matrix, -offsets[tap_inde...  22.7 us
    dot_general x8, matrix products, advance(): jnp.dot(step_gains[0], picked.astype(jnp.bfloat16), preferred_element_typ...  19.8 us
    all_gather x1, waiting for transfers between devices, shards(): gain_full = lax.all_gather(gain_rows, 'state', axis=1, tiled=True)  13.6 us
  transfers between devices with their start and end apart: 7, of which 4 were waited for; matrix products, arithmetic and copies ran while one was open for 17% of the time, Pallas kernels for 0%

commit v1 on v0

v1 whole, which is shorter than its diff:
```python
import functools

import jax
import jax.numpy as jnp
from jax import lax
from jax.experimental import pallas as pl
from jax.experimental.pallas import tpu as pltpu
from jax.sharding import PartitionSpec as P

REACH = 3
TAPS = 2 * REACH + 1
PAD = 8
LEVELS = 4
LANES = 128
CHUNK = 64
VMEM_SPEC = pl.BlockSpec(memory_space=pltpu.VMEM)


def from_behind(value, axis, steps):
    count = lax.axis_size(axis)
    return lax.ppermute(value, axis, [(source, source + steps) for source in range(count - steps)])


def dense_taps(offsets, coefficients):
    weights = coefficients / jnp.sum(coefficients, axis=0, keepdims=True)
    places = jnp.arange(-REACH, REACH + 1, dtype=offsets.dtype)
    hits = places[:, None] == offsets[None, :]
    taps = jnp.sum(jnp.where(hits[:, :, None], weights[None], 0.0), axis=1)
    return jnp.pad(taps, ((0, 8 - TAPS), (0, 0))).T


def local_gain_rows(gain_matrix, direct_gain, observed_cells):
    row_count = gain_matrix.shape[2]
    first_row = lax.axis_index("state") * row_count
    cell_ids = first_row + lax.broadcasted_iota(jnp.int32, gain_matrix.shape[2:], 0)
    observed_hit = cell_ids == observed_cells[0]
    extra = jnp.where(observed_hit, direct_gain[0], 0.0)
    return (gain_matrix[0, 0].astype(jnp.float32) + extra).astype(jnp.bfloat16)


def spread_weights(taps_ref, wide_ref):
    @pl.loop(0, wide_ref.shape[1] // CHUNK)
    def _(i):
        rows = pl.ds(pl.multiple_of(i * CHUNK, CHUNK), CHUNK)
        block = taps_ref[rows, :]
        for j in range(TAPS):
            wide_ref[j, rows, :] = jnp.broadcast_to(block[:, j : j + 1], (CHUNK, LANES))


def start_panel(x_ref, first_column):
    groups, padded, _ = x_ref.shape
    cells = padded - 2 * PAD

    @pl.loop(0, padded // PAD)
    def _(i):
        row = i * PAD - PAD + lax.broadcasted_iota(jnp.int32, (PAD, LANES), 0)
        row = jnp.where(row < 0, row + cells, jnp.where(row >= cells, row - cells, row))
        column = first_column + lax.broadcasted_iota(jnp.int32, (PAD, LANES), 1)
        rows = pl.ds(pl.multiple_of(i * PAD, PAD), PAD)
        for g in range(groups - 1):
            x_ref[g, rows, :] = (row == column + g * LANES).astype(jnp.float32)
        x_ref[groups - 1, rows, :] = jnp.zeros((PAD, LANES), jnp.float32)


def span_step(gains, cells_ref, values_ref, wide_ref, x_ref, y_ref, low_ref, hot_ref, picked_ref, store):
    groups, padded, _ = x_ref.shape
    cells = padded - 2 * PAD
    obs = picked_ref.shape[0]

    @pl.loop(0, cells // CHUNK)
    def _(i):
        base = pl.multiple_of(i * CHUNK, CHUNK)
        rows = pl.ds(base, CHUNK)
        for g in range(groups):
            total = None
            for j in range(TAPS):
                part = wide_ref[j, rows, :] * x_ref[g, pl.ds(base + (PAD - REACH + j), CHUNK), :]
                total = part if total is None else total + part
            y_ref[g, rows, :] = total
            low_ref[rows, g * LANES : (g + 1) * LANES] = total.astype(jnp.bfloat16)

    wanted = cells_ref[...]

    for b in range(cells // obs):
        ids = b * obs + lax.broadcasted_iota(jnp.int32, (obs, obs), 1)
        hot_ref[:, b * obs : (b + 1) * obs] = (ids == wanted).astype(jnp.bfloat16)
    picked_ref[:, : groups * LANES] = jnp.dot(
        hot_ref[...], low_ref[...], preferred_element_type=jnp.float32
    ).astype(jnp.bfloat16)
    lane = lax.broadcasted_iota(jnp.int32, (obs, LANES), 1)
    picked_ref[:, groups * LANES :] = jnp.where(lane == 0, -values_ref[...], 0.0).astype(jnp.bfloat16)

    block = 256

    @pl.loop(0, cells // block)
    def _(i):
        base = pl.multiple_of(i * block, block)
        rows = pl.ds(base, block)
        correction = jnp.dot(gains(base, block), picked_ref[...], preferred_element_type=jnp.float32)
        for g in range(groups):
            value = y_ref[g, rows, :] - correction[:, g * LANES : (g + 1) * LANES]
            if g == groups - 1:
                value = value - correction[:, groups * LANES :]
            store(g, base, block, value)


def compute_kernel(taps_ref, gains_ref, cells_ref, values_ref, out_ref, offset_ref,
                   wide_ref, x_ref, y_ref, low_ref, hot_ref, picked_ref):
    span = lax.axis_index("tm")
    cells = out_ref.shape[0]
    groups = x_ref.shape[0]
    first_column = lax.axis_index("state") * out_ref.shape[1]
    spread_weights(taps_ref, wide_ref)
    start_panel(x_ref, first_column)

    def keep(g, base, block, value):
        x_ref[g, pl.ds(base + PAD, block), :] = value

    def finish(g, base, block, value):
        if g < groups - 1:
            out_ref[pl.ds(base, block), g * LANES : (g + 1) * LANES] = value
        else:
            for part in range(block // LANES):
                square = value[part * LANES : (part + 1) * LANES, :].T
                offset_ref[0:1, pl.ds(pl.multiple_of(base + part * LANES, LANES), LANES)] = square[0:1, :]

    for behind in range(LEVELS - 1, -1, -1):
        def run(behind=behind):
            span_step(
                lambda base, block: gains_ref[behind, pl.ds(base, block), :],
                cells_ref.at[behind], values_ref.at[behind],
                wide_ref, x_ref, y_ref, low_ref, hot_ref, picked_ref,
                keep if behind else finish,
            )
            if behind:
                for g in range(groups):
                    x_ref[g, 0:PAD, :] = x_ref[g, cells : cells + PAD, :]
                    x_ref[g, cells + PAD : cells + 2 * PAD, :] = x_ref[g, PAD : 2 * PAD, :]

        if behind:
            pl.when(span >= behind)(run)
        else:
            run()


def shards(offsets, coefficients, gain_matrix, direct_gain, observed_cells, observed_values):
    taps = dense_taps(offsets, coefficients)
    rows = local_gain_rows(gain_matrix, direct_gain, observed_cells)
    near = lambda value: jnp.stack([value] + [from_behind(value, "tm", k) for k in range(1, LEVELS)])
    gains = lax.all_gather(near(rows), "state", axis=1, tiled=True)
    cells_used = near(observed_cells[0, 0][:, None])
    values = near(observed_values[0, 0][:, None])
    cells, obs = gains.shape[1:]
    columns = rows.shape[0]
    groups = columns // LANES + 1
    out, offset = pl.pallas_call(
        compute_kernel,
        out_shape=(
            jax.ShapeDtypeStruct((cells, columns), jnp.float32),
            jax.ShapeDtypeStruct((1, cells), jnp.float32),
        ),
        in_specs=[VMEM_SPEC] * 4,
        out_specs=(VMEM_SPEC, VMEM_SPEC),
        scratch_shapes=[
            pltpu.VMEM((TAPS, cells, LANES), jnp.float32),
            pltpu.VMEM((groups, cells + 2 * PAD, LANES), jnp.float32),
            pltpu.VMEM((groups, cells, LANES), jnp.float32),
            pltpu.VMEM((cells, groups * LANES), jnp.bfloat16),
            pltpu.VMEM((obs, cells), jnp.bfloat16),
            pltpu.VMEM((obs, (groups + 1) * LANES), jnp.bfloat16),
        ],
        compiler_params=pltpu.CompilerParams(vmem_limit_bytes=56 * 1024 * 1024),
    )(taps, gains, cells_used, values)
    return out[None], offset


def solution(mesh):
    in_specs = (
        P(),
        P(),
        P("tm", None, "state", None),
        P("tm", None, None),
        P("tm", None, None),
        P("tm", None, None),
    )
    out_specs = (P("tm", None, "state"), P("tm", None))
    return jax.shard_map(shards, mesh=mesh, in_specs=in_specs, out_specs=out_specs, check_vma=False)
```

time: 284 us -> 152 us (0.54)
  waiting for transfers between devices: 164 us -> 56 us
  Pallas kernels: 0 us -> 35.5 us
  local copies, waits for them, and re-layouts: 28.6 us -> 3.99 us
  other arithmetic: 29 us -> 8.01 us
  matrix products: 19.8 us -> 0 us
  starting transfers between devices: 22.8 us -> 33.5 us
  between operations: 17.7 us -> 14.3 us
    ppermute x6 -> x9, waiting for transfers between devices: 151 us -> 27.7 us  [from_behind(): lax.ppermute(value, axis, [(source, source + steps) for source in range(c...]
    pallas_call x0 -> x1, Pallas kernels: none -> 35.5 us  [shards(): pl.pallas_call(compute_kernel, out_shape=(jax.ShapeDtypeStruct((cells, co...]
    gather x8 -> x0, local copies, waits for them, and re-layouts: 23.6 us -> none  [advance(): picked = jnp.take(spread, cells_used[0], axis=0)]
    add x9 -> x2, other arithmetic: 22.7 us -> 0.01 us  [the longest x1 0.01 us: local_gain_rows(): first_row + lax.broadcasted_iota(jnp.int32, gain_matrix.shape[2:], 0)]
    dot_general x8 -> x0, matrix products: 19.8 us -> none  [advance(): jnp.dot(step_gains[0], picked.astype(jnp.bfloat16), preferred_element_typ...]
    all_gather x1, waiting for transfers between devices: 13.6 us -> 28.3 us  [shards(): gains = lax.all_gather(near(rows), 'state', axis=1, tiled=True)]
    ppermute x6 -> x9, starting transfers between devices: 22.8 us -> 33.5 us  [from_behind(): lax.ppermute(value, axis, [(source, source + steps) for source in range(c...]
    another operation x0 -> x3, other arithmetic: none -> 3.19 us  [shards(): jnp.stack([value] + [from_behind(value, 'tm', k) for k in range(1, LEVELS)])]
  transfers between devices with their start and end apart: 7 -> 10, of which waited for: 4 -> 4; matrix products, arithmetic and copies ran while one was open for 17% -> 6% of each run, Pallas kernels for 0% -> 0%
where the time goes in v1:
time: 152 us; the launch traced here: 151 us
  waiting for transfers between devices  56 us (37%)
  Pallas kernels  35.5 us (23%)
  starting transfers between devices  33.5 us (22%)
  between operations  14.3 us (9%)
  other arithmetic  8.01 us (5%)
  local copies, waits for them, and re-layouts  3.99 us (3%)
    pallas_call x1, Pallas kernels, shards(): pl.pallas_call(compute_kernel, out_shape=(jax.ShapeDtypeStruct((cells, co...  35.5 us
    ppermute x9, starting transfers between devices, from_behind(): lax.ppermute(value, axis, [(source, source + steps) for source in range(c...  33.5 us
    all_gather x1, waiting for transfers between devices, shards(): gains = lax.all_gather(near(rows), 'state', axis=1, tiled=True)  28.3 us
    ppermute x9, waiting for transfers between devices, from_behind(): lax.ppermute(value, axis, [(source, source + steps) for source in range(c...  27.7 us
    another operation x3, other arithmetic, shards(): jnp.stack([value] + [from_behind(value, 'tm', k) for k in range(1, LEVELS)])  3.19 us
  transfers between devices with their start and end apart: 10, of which 4 were waited for; matrix products, arithmetic and copies ran while one was open for 6% of the time, Pallas kernels for 0%

profile of v1, /device:TPU:25, one launch (start us, length us, event | category | flops | bytes accessed | tf_op | source)
XLA Modules:
  0.0 151.4 jit_solution(3476644652542632396)
XLA Ops:
  7.2 1.1 fusion.3
  8.3 4.6 %collective-permute-start.2 = (bf16[256,512]{1,0:T(8,128)(2,1)S(1)}, bf16[256,512]{1,0:T(8,128)(2,1)S(1)}, u32[]{:S(2)}, u32[]{:S(2)}) collective-permute-start(bf16[256,512]{1,0:T(8,128)(2,1)S(1)} %fusion.3), channel_id=1, source_target_pairs={{0,24},{8,32},{16,40},{24,48},{32,56},{40,64},{48,72},{56,80},{64,... | collective-permute-start | bytes 786440 | tf_op jit(solution)/shard_map/ppermute | solution.py:21
  13.0 3.3 %collective-permute-start.1 = (bf16[256,512]{1,0:T(8,128)(2,1)S(1)}, bf16[256,512]{1,0:T(8,128)(2,1)S(1)}, u32[]{:S(2)}, u32[]{:S(2)}) collective-permute-start(bf16[256,512]{1,0:T(8,128)(2,1)S(1)} %fusion.3), channel_id=1, source_target_pairs={{0,16},{8,24},{16,32},{24,40},{32,48},{40,56},{48,64},{56,72},{64,... | collective-permute-start | bytes 786440 | tf_op jit(solution)/shard_map/ppermute | solution.py:21
  16.3 3.2 %collective-permute-start = (bf16[256,512]{1,0:T(8,128)(2,1)S(1)}, bf16[256,512]{1,0:T(8,128)(2,1)S(1)}, u32[]{:S(2)}, u32[]{:S(2)}) collective-permute-start(bf16[256,512]{1,0:T(8,128)(2,1)S(1)} %fusion.3), channel_id=1, source_target_pairs={{0,8},{8,16},{16,24},{24,32},{32,40},{40,48},{48,56},{56,64},{64,7... | collective-permute-start | bytes 786440 | tf_op jit(solution)/shard_map/ppermute | solution.py:21
  19.5 1.1 fusion.1
  20.7 3.1 %collective-permute-done.2 = bf16[256,512]{1,0:T(8,128)(2,1)S(1)} collective-permute-done((bf16[256,512]{1,0:T(8,128)(2,1)S(1)}, bf16[256,512]{1,0:T(8,128)(2,1)S(1)}, u32[]{:S(2)}, u32[]{:S(2)}) %collective-permute-start.2) | collective-permute-done | bytes 262176 | tf_op jit(solution)/shard_map/ppermute | solution.py:21
  23.7 19.1 %collective-permute-done.1 = bf16[256,512]{1,0:T(8,128)(2,1)S(1)} collective-permute-done((bf16[256,512]{1,0:T(8,128)(2,1)S(1)}, bf16[256,512]{1,0:T(8,128)(2,1)S(1)}, u32[]{:S(2)}, u32[]{:S(2)}) %collective-permute-start.1) | collective-permute-done | bytes 262176 | tf_op jit(solution)/shard_map/ppermute | solution.py:21
  42.8 5.5 %collective-permute-done = bf16[256,512]{1,0:T(8,128)(2,1)S(1)} collective-permute-done((bf16[256,512]{1,0:T(8,128)(2,1)S(1)}, bf16[256,512]{1,0:T(8,128)(2,1)S(1)}, u32[]{:S(2)}, u32[]{:S(2)}) %collective-permute-start) | collective-permute-done | bytes 262176 | tf_op jit(solution)/shard_map/ppermute | solution.py:21
  48.4 1.1 pad_maximum_fusion
  49.5 3.9 %collective-permute-start.8 = (f32[512,1]{0,1:T(1,128)}, f32[512,1]{0,1:T(1,128)S(1)}, u32[]{:S(2)}, u32[]{:S(2)}) collective-permute-start(f32[512,1]{0,1:T(1,128)} %bitcast.41), channel_id=1, source_target_pairs={{0,24},{8,32},{16,40},{24,48},{32,56},{40,64},{48,72},{56,80},{64,... | collective-permute-start | bytes 6152 | tf_op jit(solution)/shard_map/ppermute | solution.py:21
  53.4 5.5 %collective-permute-start.7 = (f32[512,1]{0,1:T(1,128)}, f32[512,1]{0,1:T(1,128)S(1)}, u32[]{:S(2)}, u32[]{:S(2)}) collective-permute-start(f32[512,1]{0,1:T(1,128)} %bitcast.42), channel_id=1, source_target_pairs={{0,16},{8,24},{16,32},{24,40},{32,48},{40,56},{48,64},{56,72},{64,... | collective-permute-start | bytes 6152 | tf_op jit(solution)/shard_map/ppermute | solution.py:21
  58.9 1.9 %collective-permute-start.6 = (f32[512,1]{0,1:T(1,128)}, f32[512,1]{0,1:T(1,128)S(1)}, u32[]{:S(2)}, u32[]{:S(2)}) collective-permute-start(f32[512,1]{0,1:T(1,128)} %bitcast.43), channel_id=1, source_target_pairs={{0,8},{8,16},{16,24},{24,32},{32,40},{40,48},{48,56},{56,64},{64,7... | collective-permute-start | bytes 6152 | tf_op jit(solution)/shard_map/ppermute | solution.py:21
  60.8 4.9 %collective-permute-start.5 = (s32[512,1]{0,1:T(1,128)}, s32[512,1]{0,1:T(1,128)S(1)}, u32[]{:S(2)}, u32[]{:S(2)}) collective-permute-start(s32[512,1]{0,1:T(1,128)} %bitcast.35), channel_id=1, source_target_pairs={{0,24},{8,32},{16,40},{24,48},{32,56},{40,64},{48,72},{56,80},{64,... | collective-permute-start | bytes 6152 | tf_op jit(solution)/shard_map/ppermute | solution.py:21
  65.7 1.9 %collective-permute-start.3 = (s32[512,1]{0,1:T(1,128)}, s32[512,1]{0,1:T(1,128)S(1)}, u32[]{:S(2)}, u32[]{:S(2)}) collective-permute-start(s32[512,1]{0,1:T(1,128)} %bitcast.36), channel_id=1, source_target_pairs={{0,8},{8,16},{16,24},{24,32},{32,40},{40,48},{48,56},{56,64},{64,7... | collective-permute-start | bytes 6152 | tf_op jit(solution)/shard_map/ppermute | solution.py:21
  67.7 0.9 reduce_sum.18
  68.6 0.7 broadcast_compare_fusion
  69.3 0.9 broadcast_divide_fusion
  70.3 0.4 copy.28
  70.7 4.2 %collective-permute-start.4 = (s32[512,1]{0,1:T(1,128)}, s32[512,1]{0,1:T(1,128)S(1)}, u32[]{:S(2)}, u32[]{:S(2)}) collective-permute-start(s32[512,1]{0,1:T(1,128)} %bitcast.37), channel_id=1, source_target_pairs={{0,16},{8,24},{16,32},{24,40},{32,48},{40,56},{48,64},{56,72},{64,... | collective-permute-start | bytes 6152 | tf_op jit(solution)/shard_map/ppermute | solution.py:21
  74.9 1.1 pad_bitcast_fusion.taps_ref
  76.0 0.8 copy.29
  76.8 0.8 copy.33
  77.6 0.1 copy.30
  77.8 0.1 copy.31
  78.0 0.1 copy.32
  78.1 0.1 copy.34
  78.3 0.1 copy.35
  78.4 0.1 copy.36
  78.6 1.0 pad_add_fusion.cells_ref
  79.6 1.1 pad_maximum_fusion.1.values_ref
  80.7 28.3 %all-gather.2.cloned.1.call-done.gains_ref = bf16[4,2048,512]{2,1,0:T(8,128)(2,1)} async-done(((bf16[4,256,512]{2,1,0:T(8,128)(2,1)}), bf16[4,2048,512]{2,1,0:T(8,128)(2,1)}) %all-gather.2.cloned.1.call-update) | async-done | bytes 8388624 | tf_op jit(solution)/shard_map/all_gather | solution.py:150
  109.0 35.5 %shard_map.77 = (f32[2048,256]{1,0:T(8,128)}, f32[1,2048]{1,0:T(1,128)}) custom-call(f32[2048,8]{1,0:T(8,128)} %pad_bitcast_fusion.taps_ref, bf16[4,2048,512]{2,1,0:T(8,128)(2,1)} %all-gather.2.cloned.1.call-done.gains_ref, s32[4,512,1]{2,1,0:T(8,128)} %pad_add_fusion.cells_ref, f32[4,512,1]{2,1,0:T(8,128)} %pad_maximum_fusion.1.values_ref), custom_call_target="tpu_custom_call" | custom-call | tf_op jit(solution)/shard_map/pallas_call | solution.py:156
  (11 shorter events, 0.2 us)
Async XLA Ops:
  7.2 101.8 %all-gather.2.cloned.1.call-start = ((), (), s32[]{:S(2)}) async-start(), calls=%async_computation | async-start | bytes 9437184 | tf_op jit(solution)/shard_map/all_gather | solution.py:150
  8.3 15.4 %collective-permute-start.2 = (bf16[256,512]{1,0:T(8,128)(2,1)S(1)}, bf16[256,512]{1,0:T(8,128)(2,1)S(1)}, u32[]{:S(2)}, u32[]{:S(2)}) collective-permute-start(bf16[256,512]{1,0:T(8,128)(2,1)S(1)} %fusion.3), channel_id=1, source_target_pairs={{0,24},{8,32},{16,40},{24,48},{32,56},{40,64},{48,72},{56,80},{64,... | collective-permute-start | bytes 786440 | tf_op jit(solution)/shard_map/ppermute | solution.py:21
  13.0 29.8 %collective-permute-start.1 = (bf16[256,512]{1,0:T(8,128)(2,1)S(1)}, bf16[256,512]{1,0:T(8,128)(2,1)S(1)}, u32[]{:S(2)}, u32[]{:S(2)}) collective-permute-start(bf16[256,512]{1,0:T(8,128)(2,1)S(1)} %fusion.3), channel_id=1, source_target_pairs={{0,16},{8,24},{16,32},{24,40},{32,48},{40,56},{48,64},{56,72},{64,... | collective-permute-start | bytes 786440 | tf_op jit(solution)/shard_map/ppermute | solution.py:21
  16.3 32.0 %collective-permute-start = (bf16[256,512]{1,0:T(8,128)(2,1)S(1)}, bf16[256,512]{1,0:T(8,128)(2,1)S(1)}, u32[]{:S(2)}, u32[]{:S(2)}) collective-permute-start(bf16[256,512]{1,0:T(8,128)(2,1)S(1)} %fusion.3), channel_id=1, source_target_pairs={{0,8},{8,16},{16,24},{24,32},{32,40},{40,48},{48,56},{56,64},{64,7... | collective-permute-start | bytes 786440 | tf_op jit(solution)/shard_map/ppermute | solution.py:21
  49.5 29.0 %collective-permute-start.8 = (f32[512,1]{0,1:T(1,128)}, f32[512,1]{0,1:T(1,128)S(1)}, u32[]{:S(2)}, u32[]{:S(2)}) collective-permute-start(f32[512,1]{0,1:T(1,128)} %bitcast.41), channel_id=1, source_target_pairs={{0,24},{8,32},{16,40},{24,48},{32,56},{40,64},{48,72},{56,80},{64,... | collective-permute-start | bytes 6152 | tf_op jit(solution)/shard_map/ppermute | solution.py:21
  53.4 24.9 %collective-permute-start.7 = (f32[512,1]{0,1:T(1,128)}, f32[512,1]{0,1:T(1,128)S(1)}, u32[]{:S(2)}, u32[]{:S(2)}) collective-permute-start(f32[512,1]{0,1:T(1,128)} %bitcast.42), channel_id=1, source_target_pairs={{0,16},{8,24},{16,32},{24,40},{32,48},{40,56},{48,64},{56,72},{64,... | collective-permute-start | bytes 6152 | tf_op jit(solution)/shard_map/ppermute | solution.py:21
  58.9 19.2 %collective-permute-start.6 = (f32[512,1]{0,1:T(1,128)}, f32[512,1]{0,1:T(1,128)S(1)}, u32[]{:S(2)}, u32[]{:S(2)}) collective-permute-start(f32[512,1]{0,1:T(1,128)} %bitcast.43), channel_id=1, source_target_pairs={{0,8},{8,16},{16,24},{24,32},{32,40},{40,48},{48,56},{56,64},{64,7... | collective-permute-start | bytes 6152 | tf_op jit(solution)/shard_map/ppermute | solution.py:21
  60.8 17.1 %collective-permute-start.5 = (s32[512,1]{0,1:T(1,128)}, s32[512,1]{0,1:T(1,128)S(1)}, u32[]{:S(2)}, u32[]{:S(2)}) collective-permute-start(s32[512,1]{0,1:T(1,128)} %bitcast.35), channel_id=1, source_target_pairs={{0,24},{8,32},{16,40},{24,48},{32,56},{40,64},{48,72},{56,80},{64,... | collective-permute-start | bytes 6152 | tf_op jit(solution)/shard_map/ppermute | solution.py:21
  65.7 4.9 %collective-permute-start.3 = (s32[512,1]{0,1:T(1,128)}, s32[512,1]{0,1:T(1,128)S(1)}, u32[]{:S(2)}, u32[]{:S(2)}) collective-permute-start(s32[512,1]{0,1:T(1,128)} %bitcast.36), channel_id=1, source_target_pairs={{0,8},{8,16},{16,24},{24,32},{32,40},{40,48},{48,56},{56,64},{64,7... | collective-permute-start | bytes 6152 | tf_op jit(solution)/shard_map/ppermute | solution.py:21
  70.7 7.1 %collective-permute-start.4 = (s32[512,1]{0,1:T(1,128)}, s32[512,1]{0,1:T(1,128)S(1)}, u32[]{:S(2)}, u32[]{:S(2)}) collective-permute-start(s32[512,1]{0,1:T(1,128)} %bitcast.37), channel_id=1, source_target_pairs={{0,16},{8,24},{16,32},{24,40},{32,48},{40,56},{48,64},{56,72},{64,... | collective-permute-start | bytes 6152 | tf_op jit(solution)/shard_map/ppermute | solution.py:21
Sparse Core Ops, SparseCore 0:
  49.6 59.3 all-gather.1

commit v2 on v1

v2 whole, which is shorter than its diff:
```python
import functools

import jax
import jax.numpy as jnp
from jax import lax
from jax.experimental import pallas as pl
from jax.experimental.pallas import tpu as pltpu
from jax.sharding import PartitionSpec as P

REACH = 3
TAPS = 2 * REACH + 1
PAD = 8
LEVELS = 4
LANES = 128
CHUNK = 64
VMEM_SPEC = pl.BlockSpec(memory_space=pltpu.VMEM)

FROM_LEFT, FROM_RIGHT, FAR_LEFT, FAR_RIGHT, AHEAD, FAR_AHEAD, FACTS = range(7)
TWIN = 7
KINDS = TWIN + 7


def prepare_kernel(offsets_ref, coefficients_ref, gain_ref, direct_ref, cells_ref, values_ref,
                   rows_ref, taps_ref, facts_ref):
    row_count, obs = rows_ref.shape
    first_row = lax.axis_index("state") * row_count
    cells = cells_ref[...]

    @pl.loop(0, row_count // CHUNK)
    def _(i):
        base = pl.multiple_of(i * CHUNK, CHUNK)
        ids = first_row + base + lax.broadcasted_iota(jnp.int32, (CHUNK, obs), 0)
        extra = jnp.where(ids == cells, direct_ref[...], 0.0)
        rows_ref[pl.ds(base, CHUNK), :] = (
            gain_ref[pl.ds(base, CHUNK), :].astype(jnp.float32) + extra
        ).astype(jnp.bfloat16)

    row = lax.broadcasted_iota(jnp.int32, facts_ref.shape, 0)
    facts_ref[...] = jnp.where(row == 0, cells.astype(jnp.float32), jnp.where(row == 1, values_ref[...], 0.0))

    coefficients = coefficients_ref[...]
    weights = coefficients / jnp.sum(coefficients, axis=0, keepdims=True)
    tap = lax.broadcasted_iota(jnp.int32, (8, coefficients.shape[1]), 0)
    dense = jnp.zeros((8, coefficients.shape[1]), jnp.float32)
    for t in range(coefficients.shape[0]):
        dense = dense + jnp.where(tap == offsets_ref[t] + REACH, weights[t : t + 1, :], 0.0)
    for b in range(coefficients.shape[1] // LANES):
        taps_ref[b * LANES : (b + 1) * LANES, :] = dense[:, b * LANES : (b + 1) * LANES].T


def spread_weights(taps_ref, wide_ref):
    @pl.loop(0, wide_ref.shape[1] // CHUNK)
    def _(i):
        rows = pl.ds(pl.multiple_of(i * CHUNK, CHUNK), CHUNK)
        block = taps_ref[rows, :]
        for j in range(TAPS):
            wide_ref[j, rows, :] = jnp.broadcast_to(block[:, j : j + 1], (CHUNK, LANES))


def start_panel(x_ref, first_column):
    groups, padded, _ = x_ref.shape
    cells = padded - 2 * PAD

    @pl.loop(0, padded // PAD)
    def _(i):
        row = i * PAD - PAD + lax.broadcasted_iota(jnp.int32, (PAD, LANES), 0)
        row = jnp.where(row < 0, row + cells, jnp.where(row >= cells, row - cells, row))
        column = first_column + lax.broadcasted_iota(jnp.int32, (PAD, LANES), 1)
        rows = pl.ds(pl.multiple_of(i * PAD, PAD), PAD)
        for g in range(groups - 1):
            x_ref[g, rows, :] = (row == column + g * LANES).astype(jnp.float32)
        x_ref[groups - 1, rows, :] = jnp.zeros((PAD, LANES), jnp.float32)


def spread(wide_ref, x_ref, y_ref, low_ref):
    groups, cells, _ = y_ref.shape

    @pl.loop(0, cells // CHUNK)
    def _(i):
        base = pl.multiple_of(i * CHUNK, CHUNK)
        rows = pl.ds(base, CHUNK)
        for g in range(groups):
            total = None
            for j in range(TAPS):
                part = wide_ref[j, rows, :] * x_ref[g, pl.ds(base + (PAD - REACH + j), CHUNK), :]
                total = part if total is None else total + part
            y_ref[g, rows, :] = total
            low_ref[rows, g * LANES : (g + 1) * LANES] = total.astype(jnp.bfloat16)


def mark(facts, hot_ref, forced_ref):
    obs, cells = hot_ref.shape
    columns = facts.T
    wanted = columns[:, 0:1].astype(jnp.int32)
    for b in range(cells // obs):
        ids = b * obs + lax.broadcasted_iota(jnp.int32, (obs, obs), 1)
        hot_ref[:, b * obs : (b + 1) * obs] = (ids == wanted).astype(jnp.bfloat16)
    lane = lax.broadcasted_iota(jnp.int32, (obs, LANES), 1)
    forced_ref[...] = jnp.where(lane == 0, -columns[:, 1:2], 0.0).astype(jnp.bfloat16)


def pick(hot_ref, forced_ref, low_ref, picked_ref):
    width = low_ref.shape[1]
    picked_ref[:, :width] = jnp.dot(
        hot_ref[...], low_ref[...], preferred_element_type=jnp.float32
    ).astype(jnp.bfloat16)
    picked_ref[:, width:] = forced_ref[...]


def correct(gains_ref, picked_ref, y_ref, store):
    groups = y_ref.shape[0]
    blocks, block, _ = gains_ref.shape

    @pl.loop(0, blocks)
    def _(i):
        base = pl.multiple_of(i * block, block)
        correction = jnp.dot(gains_ref[i], picked_ref[...], preferred_element_type=jnp.float32)
        for g in range(groups):
            value = y_ref[g, pl.ds(base, block), :] - correction[:, g * LANES : (g + 1) * LANES]
            if g == groups - 1:
                value = value - correction[:, groups * LANES :]
            store(g, base, block, value)


def scan_kernel(spans, ring, taps_ref, rows_ref, facts_ref, out_ref, offset_ref,
                gains, facts, wide_ref, x_ref, y_ref, low_ref, hot_ref, forced_ref, picked_ref,
                send_sem, recv_sem, local_sem):
    span, state = lax.axis_index("tm"), lax.axis_index("state")
    chip, core = state // 2, state % 2
    place = lambda step, which: lax.rem(chip + step, ring) * 2 + which
    right, left, far = (place(step, core) for step in (1, ring - 1, 2))
    twin = place(0, 1 - core)
    twin_of = lambda step: place(step, 1 - core)
    ahead, behind_span = lax.rem(span + 1, spans), lax.rem(span + spans - 1, spans)
    count = rows_ref.shape[0]
    near = count * 3 // 16
    whole, first, second, rest = (0, count), (0, near), (near, near), (2 * near, count - 2 * near)
    cells, groups = out_ref.shape[0], x_ref.shape[0]

    barrier = pltpu.get_barrier_semaphore()
    for there in ((span, right), (span, left), (span, twin), (ahead, state), (behind_span, state)):
        pl.semaphore_signal(barrier, inc=1, device_id=there, device_id_type=pl.DeviceIdType.MESH)
    pl.semaphore_wait(barrier, 5)

    def part(k, owner, rows):
        return gains.at[k, owner, pl.ds(*rows)]

    started = []

    def send(source, target, kind, k, there):
        copy = pltpu.make_async_remote_copy(
            src_ref=source, dst_ref=target, send_sem=send_sem.at[kind, k], recv_sem=recv_sem.at[kind, k],
            device_id=there, device_id_type=pl.DeviceIdType.MESH,
        )
        copy.start()
        started.append(copy)

    def arrive(target, kind, k):
        pltpu.make_async_remote_copy(
            src_ref=target, dst_ref=target, send_sem=send_sem.at[kind, k], recv_sem=recv_sem.at[kind, k],
            device_id=(span, twin), device_id_type=pl.DeviceIdType.MESH,
        ).wait_recv()

    def to_twin(k, owner, rows, kind):
        send(part(k, owner, rows), part(k, owner, rows), TWIN + kind, k, (span, twin))

    def go_ahead(k):
        source = rows_ref if k == 0 else part(k, state, whole)
        send(facts_ref if k == 0 else facts.at[k], facts.at[k + 1], FACTS, k + 1, (ahead, state))
        send(source, part(k + 1, state, whole), AHEAD, k + 1, (ahead, state))

    def go_round(k):
        source = rows_ref if k == 0 else part(k, state, whole)
        send(source, part(k, state, whole), FROM_LEFT, k, (span, right))
        send(source, part(k, state, whole), FROM_RIGHT, k, (span, left))
        send(source, part(k, state, whole), TWIN + AHEAD, k, (span, twin))

    def take_sides(k):
        across = (first, second) if k else ((0, count // 2), (count // 2, count // 2))
        arrive(part(k, left, whole), FROM_LEFT, k)
        send(part(k, left, across[0]), part(k, left, across[0]), FAR_LEFT, k, (span, right))
        to_twin(k, left, whole, FROM_LEFT)
        arrive(part(k, right, whole), FROM_RIGHT, k)
        send(part(k, right, across[1]), part(k, right, across[1]), FAR_RIGHT, k, (span, left))
        to_twin(k, right, whole, FROM_RIGHT)

    def take_far(k):
        across = (first, second) if k else ((0, count // 2), (count // 2, count // 2))
        for rows, kind in zip(across, (FAR_LEFT, FAR_RIGHT)):
            arrive(part(k, far, rows), kind, k)
            to_twin(k, far, rows, kind)

    def far_ahead(k):
        send(part(k, far, rest), part(k + 1, far, rest), FAR_AHEAD, k + 1, (ahead, state))

    def take_far_ahead(k):
        arrive(part(k, far, rest), FAR_AHEAD, k)
        if k < LEVELS - 1:
            far_ahead(k)
        to_twin(k, far, rest, FAR_AHEAD)

    def take_ahead(k):
        arrive(facts.at[k], FACTS, k)
        arrive(part(k, state, whole), AHEAD, k)

    def take_twin(k):
        across = (first, second) if k else ((0, count // 2), (count // 2, count // 2))
        arrive(part(k, twin, whole), TWIN + AHEAD, k)
        arrive(part(k, twin_of(ring - 1), whole), TWIN + FROM_LEFT, k)
        arrive(part(k, twin_of(1), whole), TWIN + FROM_RIGHT, k)
        for rows, kind in zip(across, (FAR_LEFT, FAR_RIGHT)):
            arrive(part(k, twin_of(2), rows), TWIN + kind, k)
        if k:
            arrive(part(k, twin_of(2), rest), TWIN + FAR_AHEAD, k)

    def keep(g, base, block, value):
        x_ref[g, pl.ds(base + PAD, block), :] = value

    def finish(g, base, block, value):
        if g < groups - 1:
            out_ref[pl.ds(base, block), g * LANES : (g + 1) * LANES] = value
        else:
            for piece in range(block // LANES):
                square = value[piece * LANES : (piece + 1) * LANES, :].T
                offset_ref[0:1, pl.ds(pl.multiple_of(base + piece * LANES, LANES), LANES)] = square[0:1, :]

    def look(k):
        def run():
            spread(wide_ref, x_ref, y_ref, low_ref)
            pick(hot_ref.at[k], forced_ref.at[k], low_ref, picked_ref)

        pl.when(span >= k)(run)

    def move(k):
        def run():
            correct(gains.at[k], picked_ref, y_ref, keep if k else finish)
            if k:
                for g in range(groups):
                    x_ref[g, 0:PAD, :] = x_ref[g, cells : cells + PAD, :]
                    x_ref[g, cells + PAD : cells + 2 * PAD, :] = x_ref[g, PAD : 2 * PAD, :]

        pl.when(span >= k)(run)

    def note(k):
        mark(facts_ref[...] if k == 0 else facts[k], hot_ref.at[k], forced_ref.at[k])

    go_ahead(0)
    go_round(0)
    own = pltpu.make_async_copy(rows_ref, gains.at[0, state], local_sem)
    own.start()
    spread_weights(taps_ref, wide_ref)
    start_panel(x_ref, state * out_ref.shape[1])
    take_ahead(1)
    go_ahead(1)
    take_sides(0)
    go_round(1)
    note(0)
    note(1)
    take_far(0)
    far_ahead(0)
    take_ahead(2)
    go_ahead(2)
    note(2)
    take_sides(1)
    take_ahead(3)
    go_round(3)
    note(3)
    take_far_ahead(1)
    take_far(1)
    look(3)
    take_sides(3)
    go_round(2)
    take_far_ahead(2)
    take_far_ahead(3)
    take_far(3)
    take_twin(3)
    move(3)
    take_sides(2)
    look(2)
    take_far(2)
    take_twin(2)
    move(2)
    look(1)
    take_twin(1)
    move(1)
    look(0)
    own.wait()
    take_twin(0)
    move(0)
    for copy in started:
        copy.wait_send()


def shards(spans, states, offsets, coefficients, gain_matrix, direct_gain, observed_cells, observed_values):
    row_count, obs = gain_matrix.shape[2:]
    cells = coefficients.shape[1]
    rows, taps, facts = pl.pallas_call(
        prepare_kernel,
        out_shape=(
            jax.ShapeDtypeStruct((row_count, obs), jnp.bfloat16),
            jax.ShapeDtypeStruct((cells, 8), jnp.float32),
            jax.ShapeDtypeStruct((8, obs), jnp.float32),
        ),
        in_specs=[pl.BlockSpec(memory_space=pltpu.SMEM)] + [VMEM_SPEC] * 5,
        out_specs=(VMEM_SPEC,) * 3,
        name="prepare",
    )(offsets, coefficients, gain_matrix[0, 0], direct_gain[0], observed_cells[0], observed_values[0])
    groups = row_count // LANES + 1
    out, offset = pl.pallas_call(
        functools.partial(scan_kernel, spans, states // 2),
        out_shape=(
            jax.ShapeDtypeStruct((cells, row_count), jnp.float32),
            jax.ShapeDtypeStruct((1, cells), jnp.float32),
        ),
        in_specs=[VMEM_SPEC] * 3,
        out_specs=(VMEM_SPEC, VMEM_SPEC),
        scratch_shapes=[
            pltpu.VMEM((LEVELS, states, row_count, obs), jnp.bfloat16),
            pltpu.VMEM((LEVELS, 8, obs), jnp.float32),
            pltpu.VMEM((TAPS, cells, LANES), jnp.float32),
            pltpu.VMEM((groups, cells + 2 * PAD, LANES), jnp.float32),
            pltpu.VMEM((groups, cells, LANES), jnp.float32),
            pltpu.VMEM((cells, groups * LANES), jnp.bfloat16),
            pltpu.VMEM((LEVELS, obs, cells), jnp.bfloat16),
            pltpu.VMEM((LEVELS, obs, LANES), jnp.bfloat16),
            pltpu.VMEM((obs, (groups + 1) * LANES), jnp.bfloat16),
            pltpu.SemaphoreType.DMA((KINDS, LEVELS)),
            pltpu.SemaphoreType.DMA((KINDS, LEVELS)),
            pltpu.SemaphoreType.DMA,
        ],
        compiler_params=pltpu.CompilerParams(
            collective_id=0, has_side_effects=True, vmem_limit_bytes=56 * 1024 * 1024
        ),
        name="scan",
    )(taps, rows, facts)
    return out[None], offset


def solution(mesh):
    in_specs = (
        P(),
        P(),
        P("tm", None, "state", None),
        P("tm", None, None),
        P("tm", None, None),
        P("tm", None, None),
    )
    out_specs = (P("tm", None, "state"), P("tm", None))
    run = functools.partial(shards, mesh.shape["tm"], mesh.shape["state"])
    return jax.shard_map(run, mesh=mesh, in_specs=in_specs, out_specs=out_specs, check_vma=False)
```

time: 152 us -> 80.2 us (0.53)
  waiting for transfers between devices: 56 us -> 0 us
  Pallas kernels: 35.5 us -> 75.1 us
  starting transfers between devices: 33.5 us -> 0 us
  between operations: 14.3 us -> 0.65 us
  other arithmetic: 8.01 us -> 0 us
    pallas_call x1 -> x2, Pallas kernels: 35.5 us -> 75.1 us  [the longest x1 72.7 us: shards(): pl.pallas_call(functools.partial(scan_kernel, spans, states // 2), out_sh...]
    ppermute x9 -> x0, starting transfers between devices: 33.5 us -> none  [from_behind(): lax.ppermute(value, axis, [(source, source + steps) for source in range(c...]
    all_gather x1 -> x0, waiting for transfers between devices: 28.3 us -> none  [shards(): gains = lax.all_gather(near(rows), 'state', axis=1, tiled=True)]
    ppermute x9 -> x0, waiting for transfers between devices: 27.7 us -> none  [from_behind(): lax.ppermute(value, axis, [(source, source + steps) for source in range(c...]
    unnamed x0 -> x4, local copies, waits for them, and re-layouts: none -> 3.65 us
    another operation x3 -> x0, other arithmetic: 3.19 us -> none  [shards(): jnp.stack([value] + [from_behind(value, 'tm', k) for k in range(1, LEVELS)])]
    another operation x8 -> x0, local copies, waits for them, and re-layouts: 2.52 us -> none  [shards(): jnp.stack([value] + [from_behind(value, 'tm', k) for k in range(1, LEVELS)])]
    convert_element_type x2 -> x0, other arithmetic: 2.23 us -> none  [local_gain_rows(): return (gain_matrix[0, 0].astype(jnp.float32) + extra).astype(jnp.bfloat16)]
  transfers between devices with their start and end apart: 10 -> 0, of which waited for: 4 -> 0; matrix products, arithmetic and copies ran while one was open for 6% -> 0% of each run, Pallas kernels for 0% -> 0%
where the time goes in v2:
time: 80.2 us; the launch traced here: 79.4 us
  Pallas kernels  75.1 us (94%)
  local copies, waits for them, and re-layouts  3.65 us (5%)
    pallas_call x1, Pallas kernels, shards(): pl.pallas_call(functools.partial(scan_kernel, spans, states // 2), out_sh...  72.7 us
    unnamed x4, local copies, waits for them, and re-layouts  3.65 us
    pallas_call x1, Pallas kernels, shards(): pl.pallas_call(prepare_kernel, out_shape=(jax.ShapeDtypeStruct((row_count...  2.4 us

profile of v2, /device:TPU:25, one launch (start us, length us, event | category | flops | bytes accessed | tf_op | source)
XLA Modules:
  0.0 79.4 jit_solution(9942506952557460879)
XLA Ops:
  0.6 2.4 %prepare.1 = (bf16[256,512]{1,0:T(8,128)(2,1)}, f32[2048,8]{1,0:T(8,128)}, f32[8,512]{1,0:T(8,128)}) custom-call(s32[5]{0:T(128)} %offsets_ref.1, f32[5,2048]{1,0:T(8,128)} %coefficients_ref.1, bf16[256,512]{1,0:T(8,128)(2,1)} %bitcast.6, f32[1,512]{1,0:T(1,128)} %bitcast.7, s32[1,512]{1,0:T(1,128)} %bitcast.8, f32[1,512]{1,0:T(1,128)} %bitcast.9), custom_call_target="tpu_custom_call" | custom-call | tf_op jit(solution)/shard_map/prepare/pallas_call | solution.py:297
  3.0 72.7 %scan.1 = (f32[2048,256]{1,0:T(8,128)}, f32[1,2048]{1,0:T(1,128)}) custom-call(f32[2048,8]{1,0:T(8,128)} %get-tuple-element.7.taps_ref, bf16[256,512]{1,0:T(8,128)(2,1)} %get-tuple-element.8.rows_ref, f32[8,512]{1,0:T(8,128)} %get-tuple-element.9.facts_ref), custom_call_target="tpu_custom_call" | custom-call | tf_op jit(solution)/shard_map/scan/pallas_call | solution.py:309
  75.7 0.0 copy-start
  75.7 3.0 %copy.10 = f32[1,2048,256]{2,1,0:T(8,128)} copy(f32[1,2048,256]{2,1,0:T(8,128)} %bitcast.5) | data formatting | bytes 4194304
  78.8 0.0 copy-done
  78.8 0.6 copy.11
Async XLA Ops:
  75.7 3.1 %copy-start = (f32[1,2048]{1,0:T(1,128)S(1)}, f32[1,2048]{1,0:T(1,128)}, u32[]{:S(2)}) copy-start(f32[1,2048]{1,0:T(1,128)} %get-tuple-element.15) | copy-start | bytes 24580

commit v3 on v2

--- a/solution.py
+++ b/solution.py
@@ -15,7 +15,7 @@
 CHUNK = 64
 VMEM_SPEC = pl.BlockSpec(memory_space=pltpu.VMEM)
 
-FROM_LEFT, FROM_RIGHT, FAR_LEFT, FAR_RIGHT, AHEAD, FAR_AHEAD, FACTS = range(7)
+FROM_LEFT, FROM_RIGHT, FAR_LEFT, FAR_RIGHT, AHEAD, AHEAD_LATE, FACTS = range(7)
 TWIN = 7
 KINDS = TWIN + 7
 
@@ -133,8 +133,8 @@
     twin_of = lambda step: place(step, 1 - core)
     ahead, behind_span = lax.rem(span + 1, spans), lax.rem(span + spans - 1, spans)
     count = rows_ref.shape[0]
-    near = count * 3 // 16
-    whole, first, second, rest = (0, count), (0, near), (near, near), (2 * near, count - 2 * near)
+    half = count // 2
+    whole, halves = (0, count), ((0, half), (half, half))
     cells, groups = out_ref.shape[0], x_ref.shape[0]
 
     barrier = pltpu.get_barrier_semaphore()
@@ -164,10 +164,19 @@
     def to_twin(k, owner, rows, kind):
         send(part(k, owner, rows), part(k, owner, rows), TWIN + kind, k, (span, twin))
 
-    def go_ahead(k):
-        source = rows_ref if k == 0 else part(k, state, whole)
-        send(facts_ref if k == 0 else facts.at[k], facts.at[k + 1], FACTS, k + 1, (ahead, state))
-        send(source, part(k + 1, state, whole), AHEAD, k + 1, (ahead, state))
+    def go_ahead(k, h):
+        rows = halves[h]
+        source = rows_ref.at[pl.ds(*rows)] if k == 0 else part(k, state, rows)
+        if h == 0:
+            send(facts_ref if k == 0 else facts.at[k], facts.at[k + 1], FACTS, k + 1, (ahead, state))
+        send(source, part(k + 1, state, rows), AHEAD + h, k + 1, (ahead, state))
+
+    def take_ahead(k, h):
+        if h == 0:
+            arrive(facts.at[k], FACTS, k)
+        arrive(part(k, state, halves[h]), AHEAD + h, k)
+        if k < LEVELS - 1:
+            go_ahead(k, h)
 
     def go_round(k):
         source = rows_ref if k == 0 else part(k, state, whole)
@@ -176,42 +185,25 @@
         send(source, part(k, state, whole), TWIN + AHEAD, k, (span, twin))
 
     def take_sides(k):
-        across = (first, second) if k else ((0, count // 2), (count // 2, count // 2))
-        arrive(part(k, left, whole), FROM_LEFT, k)
-        send(part(k, left, across[0]), part(k, left, across[0]), FAR_LEFT, k, (span, right))
-        to_twin(k, left, whole, FROM_LEFT)
-        arrive(part(k, right, whole), FROM_RIGHT, k)
-        send(part(k, right, across[1]), part(k, right, across[1]), FAR_RIGHT, k, (span, left))
-        to_twin(k, right, whole, FROM_RIGHT)
+        for owner, kind in ((left, FROM_LEFT), (right, FROM_RIGHT)):
+            arrive(part(k, owner, whole), kind, k)
+            to_twin(k, owner, whole, kind)
+
+    def relay(k):
+        send(part(k, left, halves[0]), part(k, left, halves[0]), FAR_LEFT, k, (span, right))
+        send(part(k, right, halves[1]), part(k, right, halves[1]), FAR_RIGHT, k, (span, left))
 
     def take_far(k):
-        across = (first, second) if k else ((0, count // 2), (count // 2, count // 2))
-        for rows, kind in zip(across, (FAR_LEFT, FAR_RIGHT)):
+        for rows, kind in zip(halves, (FAR_LEFT, FAR_RIGHT)):
             arrive(part(k, far, rows), kind, k)
             to_twin(k, far, rows, kind)
 
-    def far_ahead(k):
-        send(part(k, far, rest), part(k + 1, far, rest), FAR_AHEAD, k + 1, (ahead, state))
-
-    def take_far_ahead(k):
-        arrive(part(k, far, rest), FAR_AHEAD, k)
-        if k < LEVELS - 1:
-            far_ahead(k)
-        to_twin(k, far, rest, FAR_AHEAD)
-
-    def take_ahead(k):
-        arrive(facts.at[k], FACTS, k)
-        arrive(part(k, state, whole), AHEAD, k)
-
     def take_twin(k):
-        across = (first, second) if k else ((0, count // 2), (count // 2, count // 2))
         arrive(part(k, twin, whole), TWIN + AHEAD, k)
         arrive(part(k, twin_of(ring - 1), whole), TWIN + FROM_LEFT, k)
         arrive(part(k, twin_of(1), whole), TWIN + FROM_RIGHT, k)
-        for rows, kind in zip(across, (FAR_LEFT, FAR_RIGHT)):
+        for rows, kind in zip(halves, (FAR_LEFT, FAR_RIGHT)):
             arrive(part(k, twin_of(2), rows), TWIN + kind, k)
-        if k:
-            arrive(part(k, twin_of(2), rest), TWIN + FAR_AHEAD, k)
 
     def keep(g, base, block, value):
         x_ref[g, pl.ds(base + PAD, block), :] = value
@@ -244,42 +236,44 @@
     def note(k):
         mark(facts_ref[...] if k == 0 else facts[k], hot_ref.at[k], forced_ref.at[k])
 
-    go_ahead(0)
+    go_ahead(0, 0)
+    go_ahead(0, 1)
     go_round(0)
     own = pltpu.make_async_copy(rows_ref, gains.at[0, state], local_sem)
     own.start()
     spread_weights(taps_ref, wide_ref)
+    take_ahead(1, 0)
     start_panel(x_ref, state * out_ref.shape[1])
-    take_ahead(1)
-    go_ahead(1)
+    note(0)
+    take_ahead(1, 1)
+    go_round(1)
     take_sides(0)
-    go_round(1)
-    note(0)
     note(1)
-    take_far(0)
-    far_ahead(0)
-    take_ahead(2)
-    go_ahead(2)
+    take_ahead(2, 0)
     note(2)
+    take_ahead(2, 1)
+    go_round(2)
     take_sides(1)
-    take_ahead(3)
+    take_ahead(3, 0)
+    note(3)
+    take_ahead(3, 1)
     go_round(3)
-    note(3)
-    take_far_ahead(1)
-    take_far(1)
+    take_sides(2)
+    relay(2)
     look(3)
     take_sides(3)
-    go_round(2)
-    take_far_ahead(2)
-    take_far_ahead(3)
+    relay(3)
+    relay(1)
+    relay(0)
+    take_far(2)
     take_far(3)
     take_twin(3)
     move(3)
-    take_sides(2)
+    take_far(1)
     look(2)
-    take_far(2)
     take_twin(2)
     move(2)
+    take_far(0)
     look(1)
     take_twin(1)
     move(1)

time: 80.2 us -> 76.3 us (0.951)
  Pallas kernels: 75.1 us -> 71.7 us
    pallas_call x1, Pallas kernels: 72.7 us -> 69.3 us  [shards(): pl.pallas_call(functools.partial(scan_kernel, spans, states // 2), out_sh...]
where the time goes in v3:
time: 76.3 us; the launch traced here: 76 us
  Pallas kernels  71.7 us (94%)
  local copies, waits for them, and re-layouts  3.65 us (5%)
    pallas_call x1, Pallas kernels, shards(): pl.pallas_call(functools.partial(scan_kernel, spans, states // 2), out_sh...  69.3 us
    unnamed x4, local copies, waits for them, and re-layouts  3.65 us
    pallas_call x1, Pallas kernels, shards(): pl.pallas_call(prepare_kernel, out_shape=(jax.ShapeDtypeStruct((row_count...  2.4 us

profile of v3, /device:TPU:25, one launch (start us, length us, event | category | flops | bytes accessed | tf_op | source)
XLA Modules:
  0.0 76.0 jit_solution(2757035172503734373)
XLA Ops:
  0.6 2.4 %prepare.1 = (bf16[256,512]{1,0:T(8,128)(2,1)}, f32[2048,8]{1,0:T(8,128)}, f32[8,512]{1,0:T(8,128)}) custom-call(s32[5]{0:T(128)} %offsets_ref.1, f32[5,2048]{1,0:T(8,128)} %coefficients_ref.1, bf16[256,512]{1,0:T(8,128)(2,1)} %bitcast.6, f32[1,512]{1,0:T(1,128)} %bitcast.7, s32[1,512]{1,0:T(1,128)} %bitcast.8, f32[1,512]{1,0:T(1,128)} %bitcast.9), custom_call_target="tpu_custom_call" | custom-call | tf_op jit(solution)/shard_map/prepare/pallas_call | solution.py:291
  3.0 69.3 %scan.1 = (f32[2048,256]{1,0:T(8,128)}, f32[1,2048]{1,0:T(1,128)}) custom-call(f32[2048,8]{1,0:T(8,128)} %get-tuple-element.7.taps_ref, bf16[256,512]{1,0:T(8,128)(2,1)} %get-tuple-element.8.rows_ref, f32[8,512]{1,0:T(8,128)} %get-tuple-element.9.facts_ref), custom_call_target="tpu_custom_call" | custom-call | tf_op jit(solution)/shard_map/scan/pallas_call | solution.py:303
  72.3 0.0 copy-start
  72.3 3.0 %copy.10 = f32[1,2048,256]{2,1,0:T(8,128)} copy(f32[1,2048,256]{2,1,0:T(8,128)} %bitcast.5) | data formatting | bytes 4194304
  75.4 0.0 copy-done
  75.4 0.6 copy.11
Async XLA Ops:
  72.3 3.1 %copy-start = (f32[1,2048]{1,0:T(1,128)S(1)}, f32[1,2048]{1,0:T(1,128)}, u32[]{:S(2)}) copy-start(f32[1,2048]{1,0:T(1,128)} %get-tuple-element.15) | copy-start | bytes 24580

commit v4 on v3

--- a/solution.py
+++ b/solution.py
@@ -48,8 +48,10 @@
         taps_ref[b * LANES : (b + 1) * LANES, :] = dense[:, b * LANES : (b + 1) * LANES].T
 
 
-def spread_weights(taps_ref, wide_ref):
-    @pl.loop(0, wide_ref.shape[1] // CHUNK)
+def spread_weights(quarter, taps_ref, wide_ref):
+    chunks = wide_ref.shape[1] // CHUNK // 4
+
+    @pl.loop(quarter * chunks, (quarter + 1) * chunks)
     def _(i):
         rows = pl.ds(pl.multiple_of(i * CHUNK, CHUNK), CHUNK)
         block = taps_ref[rows, :]
@@ -236,43 +238,49 @@
     def note(k):
         mark(facts_ref[...] if k == 0 else facts[k], hot_ref.at[k], forced_ref.at[k])
 
+    def widen(quarter):
+        spread_weights(quarter, taps_ref, wide_ref)
+
     go_ahead(0, 0)
     go_ahead(0, 1)
     go_round(0)
     own = pltpu.make_async_copy(rows_ref, gains.at[0, state], local_sem)
     own.start()
-    spread_weights(taps_ref, wide_ref)
-    take_ahead(1, 0)
     start_panel(x_ref, state * out_ref.shape[1])
     note(0)
+    widen(0)
+    take_ahead(1, 0)
+    widen(1)
     take_ahead(1, 1)
     go_round(1)
     take_sides(0)
     note(1)
     take_ahead(2, 0)
-    note(2)
+    widen(2)
     take_ahead(2, 1)
     go_round(2)
+    note(2)
     take_sides(1)
     take_ahead(3, 0)
-    note(3)
+    widen(3)
     take_ahead(3, 1)
     go_round(3)
+    note(3)
     take_sides(2)
-    relay(2)
     look(3)
     take_sides(3)
     relay(3)
+    relay(2)
     relay(1)
     relay(0)
-    take_far(2)
     take_far(3)
     take_twin(3)
     move(3)
-    take_far(1)
+    take_far(2)
     look(2)
     take_twin(2)
     move(2)
+    take_far(1)
     take_far(0)
     look(1)
     take_twin(1)
@@ -283,6 +291,23 @@
     move(0)
     for copy in started:
         copy.wait_send()
+
+
+def deliver_kernel(out_ref, offset_ref, out_final_ref, offset_final_ref, block_ref, line_ref, in_sem, done_sem):
+    blocks, rows, _ = block_ref.shape
+    pieces = [
+        (out_ref.at[pl.ds(b * rows, rows)], block_ref.at[b], out_final_ref.at[pl.ds(b * rows, rows)])
+        for b in range(blocks)
+    ] + [(offset_ref, line_ref, offset_final_ref)]
+    taken = [pltpu.make_async_copy(a, b, in_sem.at[n]) for n, (a, b, _) in enumerate(pieces)]
+    given = [pltpu.make_async_copy(b, c, done_sem.at[n]) for n, (_, b, c) in enumerate(pieces)]
+    for copy in taken:
+        copy.start()
+    for before, after in zip(taken, given):
+        before.wait()
+        after.start()
+    for copy in given:
+        copy.wait()
 
 
 def shards(spans, states, offsets, coefficients, gain_matrix, direct_gain, observed_cells, observed_values):
@@ -327,6 +352,24 @@
         ),
         name="scan",
     )(taps, rows, facts)
+    anywhere = pl.BlockSpec(memory_space=pl.ANY)
+    blocks = 8
+    out, offset = pl.pallas_call(
+        deliver_kernel,
+        out_shape=(
+            jax.ShapeDtypeStruct(out.shape, out.dtype),
+            jax.ShapeDtypeStruct(offset.shape, offset.dtype),
+        ),
+        in_specs=[anywhere] * 2,
+        out_specs=(anywhere,) * 2,
+        scratch_shapes=[
+            pltpu.VMEM((blocks, cells // blocks, row_count), jnp.float32),
+            pltpu.VMEM(offset.shape, jnp.float32),
+            pltpu.SemaphoreType.DMA((blocks + 1,)),
+            pltpu.SemaphoreType.DMA((blocks + 1,)),
+        ],
+        name="deliver",
+    )(out, offset)
     return out[None], offset
 
 

time: 76.3 us -> 74 us (0.970)
  local copies, waits for them, and re-layouts: 3.65 us -> 0 us
  Pallas kernels: 71.7 us -> 73.2 us
    unnamed x4 -> x0, local copies, waits for them, and re-layouts: 3.65 us -> none
    pallas_call x0 -> x1, Pallas kernels: none -> 2.41 us  [shards(): pl.pallas_call(deliver_kernel, out_shape=(jax.ShapeDtypeStruct(out.shape,...]
    pallas_call x1, Pallas kernels: 69.3 us -> 68.3 us  [shards(): pl.pallas_call(functools.partial(scan_kernel, spans, states // 2), out_sh...]
where the time goes in v4:
time: 74 us; the launch traced here: 73.8 us
  Pallas kernels  73.2 us (99%)
    pallas_call x1, Pallas kernels, shards(): pl.pallas_call(functools.partial(scan_kernel, spans, states // 2), out_sh...  68.3 us
    pallas_call x1, Pallas kernels, shards(): pl.pallas_call(deliver_kernel, out_shape=(jax.ShapeDtypeStruct(out.shape,...  2.41 us
    pallas_call x1, Pallas kernels, shards(): pl.pallas_call(prepare_kernel, out_shape=(jax.ShapeDtypeStruct((row_count...  2.4 us

profile of v4, /device:TPU:25, one launch (start us, length us, event | category | flops | bytes accessed | tf_op | source)
XLA Modules:
  0.0 73.8 jit_solution(16410501171511683124)
XLA Ops:
  0.6 2.4 %prepare.1 = (bf16[256,512]{1,0:T(8,128)(2,1)}, f32[2048,8]{1,0:T(8,128)}, f32[8,512]{1,0:T(8,128)}) custom-call(s32[5]{0:T(128)} %offsets_ref.1, f32[5,2048]{1,0:T(8,128)} %coefficients_ref.1, bf16[256,512]{1,0:T(8,128)(2,1)} %bitcast.5, f32[1,512]{1,0:T(1,128)} %bitcast.6, s32[1,512]{1,0:T(1,128)} %bitcast.7, f32[1,512]{1,0:T(1,128)} %bitcast.8), custom_call_target="tpu_custom_call" | custom-call | tf_op jit(solution)/shard_map/prepare/pallas_call | solution.py:316
  3.0 68.3 %scan.1 = (f32[2048,256]{1,0:T(8,128)}, f32[1,2048]{1,0:T(1,128)}) custom-call(f32[2048,8]{1,0:T(8,128)} %get-tuple-element.9.taps_ref, bf16[256,512]{1,0:T(8,128)(2,1)} %get-tuple-element.10.rows_ref, f32[8,512]{1,0:T(8,128)} %get-tuple-element.11.facts_ref), custom_call_target="tpu_custom_call" | custom-call | tf_op jit(solution)/shard_map/scan/pallas_call | solution.py:328
  71.4 2.4 %deliver.1 = (f32[2048,256]{1,0:T(8,128)}, f32[1,2048]{1,0:T(1,128)}) custom-call(f32[2048,256]{1,0:T(8,128)} %get-tuple-element.12.out_ref, f32[1,2048]{1,0:T(1,128)} %get-tuple-element.13.offset_ref), custom_call_target="tpu_custom_call" | custom-call | tf_op jit(solution)/shard_map/deliver/pallas_call | solution.py:357

commit v5 on v4

--- a/solution.py
+++ b/solution.py
@@ -15,9 +15,9 @@
 CHUNK = 64
 VMEM_SPEC = pl.BlockSpec(memory_space=pltpu.VMEM)
 
-FROM_LEFT, FROM_RIGHT, FAR_LEFT, FAR_RIGHT, AHEAD, AHEAD_LATE, FACTS = range(7)
-TWIN = 7
-KINDS = TWIN + 7
+FROM_LEFT, FROM_RIGHT, FAR_LEFT, FAR_RIGHT, AHEAD, AHEAD_LATE, FACTS, FAR_AHEAD = range(8)
+TWIN = 8
+KINDS = TWIN + 8
 
 
 def prepare_kernel(offsets_ref, coefficients_ref, gain_ref, direct_ref, cells_ref, values_ref,
@@ -137,6 +137,7 @@
     count = rows_ref.shape[0]
     half = count // 2
     whole, halves = (0, count), ((0, half), (half, half))
+    quarters, rest = ((0, half // 2), (half // 2, half // 2)), halves[1]
     cells, groups = out_ref.shape[0], x_ref.shape[0]
 
     barrier = pltpu.get_barrier_semaphore()
@@ -192,11 +193,21 @@
             to_twin(k, owner, whole, kind)
 
     def relay(k):
-        send(part(k, left, halves[0]), part(k, left, halves[0]), FAR_LEFT, k, (span, right))
-        send(part(k, right, halves[1]), part(k, right, halves[1]), FAR_RIGHT, k, (span, left))
+        first, second = quarters if k else halves
+        send(part(k, left, first), part(k, left, first), FAR_LEFT, k, (span, right))
+        send(part(k, right, second), part(k, right, second), FAR_RIGHT, k, (span, left))
+
+    def far_ahead(k):
+        send(part(k, far, rest), part(k + 1, far, rest), FAR_AHEAD, k + 1, (ahead, state))
+
+    def take_far_ahead(k):
+        arrive(part(k, far, rest), FAR_AHEAD, k)
+        if k < LEVELS - 1:
+            far_ahead(k)
+        to_twin(k, far, rest, FAR_AHEAD)
 
     def take_far(k):
-        for rows, kind in zip(halves, (FAR_LEFT, FAR_RIGHT)):
+        for rows, kind in zip(quarters if k else halves, (FAR_LEFT, FAR_RIGHT)):
             arrive(part(k, far, rows), kind, k)
             to_twin(k, far, rows, kind)
 
@@ -204,8 +215,10 @@
         arrive(part(k, twin, whole), TWIN + AHEAD, k)
         arrive(part(k, twin_of(ring - 1), whole), TWIN + FROM_LEFT, k)
         arrive(part(k, twin_of(1), whole), TWIN + FROM_RIGHT, k)
-        for rows, kind in zip(halves, (FAR_LEFT, FAR_RIGHT)):
+        for rows, kind in zip(quarters if k else halves, (FAR_LEFT, FAR_RIGHT)):
             arrive(part(k, twin_of(2), rows), TWIN + kind, k)
+        if k:
+            arrive(part(k, twin_of(2), rest), TWIN + FAR_AHEAD, k)
 
     def keep(g, base, block, value):
         x_ref[g, pl.ds(base + PAD, block), :] = value
@@ -254,6 +267,7 @@
     take_ahead(1, 1)
     go_round(1)
     take_sides(0)
+    relay(0)
     note(1)
     take_ahead(2, 0)
     widen(2)
@@ -265,15 +279,19 @@
     widen(3)
     take_ahead(3, 1)
     go_round(3)
+    take_far(0)
+    far_ahead(0)
     note(3)
     take_sides(2)
     look(3)
+    take_far_ahead(1)
     take_sides(3)
     relay(3)
     relay(2)
     relay(1)
-    relay(0)
+    take_far_ahead(2)
     take_far(3)
+    take_far_ahead(3)
     take_twin(3)
     move(3)
     take_far(2)
@@ -281,7 +299,6 @@
     take_twin(2)
     move(2)
     take_far(1)
-    take_far(0)
     look(1)
     take_twin(1)
     move(1)

time: 74 us -> 77.5 us (1.047)
  Pallas kernels: 73.2 us -> 76.7 us
    pallas_call x1, Pallas kernels: 68.3 us -> 71.8 us  [shards(): pl.pallas_call(functools.partial(scan_kernel, spans, states // 2), out_sh...]
where the time goes in v5:
time: 77.5 us; the launch traced here: 77.3 us
  Pallas kernels  76.7 us (99%)
    pallas_call x1, Pallas kernels, shards(): pl.pallas_call(functools.partial(scan_kernel, spans, states // 2), out_sh...  71.8 us
    pallas_call x1, Pallas kernels, shards(): pl.pallas_call(deliver_kernel, out_shape=(jax.ShapeDtypeStruct(out.shape,...  2.41 us
    pallas_call x1, Pallas kernels, shards(): pl.pallas_call(prepare_kernel, out_shape=(jax.ShapeDtypeStruct((row_count...  2.4 us

profile of v5, /device:TPU:25, one launch (start us, length us, event | category | flops | bytes accessed | tf_op | source)
XLA Modules:
  0.0 77.3 jit_solution(6947848033013797234)
XLA Ops:
  0.6 2.4 %prepare.1 = (bf16[256,512]{1,0:T(8,128)(2,1)}, f32[2048,8]{1,0:T(8,128)}, f32[8,512]{1,0:T(8,128)}) custom-call(s32[5]{0:T(128)} %offsets_ref.1, f32[5,2048]{1,0:T(8,128)} %coefficients_ref.1, bf16[256,512]{1,0:T(8,128)(2,1)} %bitcast.5, f32[1,512]{1,0:T(1,128)} %bitcast.6, s32[1,512]{1,0:T(1,128)} %bitcast.7, f32[1,512]{1,0:T(1,128)} %bitcast.8), custom_call_target="tpu_custom_call" | custom-call | tf_op jit(solution)/shard_map/prepare/pallas_call | solution.py:333
  3.0 71.8 %scan.1 = (f32[2048,256]{1,0:T(8,128)}, f32[1,2048]{1,0:T(1,128)}) custom-call(f32[2048,8]{1,0:T(8,128)} %get-tuple-element.9.taps_ref, bf16[256,512]{1,0:T(8,128)(2,1)} %get-tuple-element.10.rows_ref, f32[8,512]{1,0:T(8,128)} %get-tuple-element.11.facts_ref), custom_call_target="tpu_custom_call" | custom-call | tf_op jit(solution)/shard_map/scan/pallas_call | solution.py:345
  74.9 2.4 %deliver.1 = (f32[2048,256]{1,0:T(8,128)}, f32[1,2048]{1,0:T(1,128)}) custom-call(f32[2048,256]{1,0:T(8,128)} %get-tuple-element.12.out_ref, f32[1,2048]{1,0:T(1,128)} %get-tuple-element.13.offset_ref), custom_call_target="tpu_custom_call" | custom-call | tf_op jit(solution)/shard_map/deliver/pallas_call | solution.py:374
